TPU v7x, 32 devices: a whole 2x2x4 slice. The times are simulated.
32 devices in a mesh: grp: 4 (over y, x), seq: 8 (over z, core).
Axes of the slice: x: 2, y: 2, z: 4, core: 2. Of those that a mesh axis runs over, the one named last changes fastest.
Arguments:
- queries: bfloat16 [1024, 64, 192], P('seq', 'grp'), may hold values from -6 to 6
- key_cache: bfloat16 [4, 8192, 192], P('grp', 'seq'), may hold values from -6 to 6
- group_value_cache: bfloat16 [4, 8192, 128], P('grp', 'seq'), may hold values from -6 to 6
- coarse_keys: bfloat16 [4, 512, 192], P('grp', 'seq'), may hold values from -6 to 6
- coarse_values: bfloat16 [4, 512, 128], P('grp', 'seq'), may hold values from -6 to 6
- hidden: bfloat16 [1024, 2560], P('seq'), may hold values from -6 to 6
- gate_weight: bfloat16 [4, 2560, 32], P('grp'), may hold values from -0.125 to 0.125
- out_weight: bfloat16 [8192, 2560], P('grp'), may hold values from -0.09375 to 0.09375
- selected: int32 [4, 8, 16], P('grp', 'seq'), may hold values from 0 to 127, as said below
Outputs:
- layer_out: bfloat16 [1024, 2560], P('seq', 'grp')
Inputs may be any that keep to these rules, and one draw needn't show every extreme that they name: selected[g, t] lists 16 distinct blocks of 64 positions for tile t of group g; the first is block 0; none starts after the tile's last query position; at most 4 of them lie within one index of seq's 1024 positions.
All inputs are finite; a program needn't handle non-finite values.
Results may differ from a plain program's by a relative error of at most 0.013.
Values may be sent and summed in bfloat16 or wider, within the bound.
A program may use at most 128 MiB of HBM per device.

v0:
```python
import functools
import math

import jax
import jax.numpy as jnp
from jax import lax
from jax.experimental import pallas as pl
from jax.experimental.pallas import tpu as pltpu
from jax.sharding import PartitionSpec as P

BLK = 64
SEL = 16
TILE = 128
CSTRIDE = 16
CLEN = 32

NEGATIVE = -1e30
FAR = 1 << 28
MESH = pl.DeviceIdType.MESH
HALF = BLK // 2
UNIT = BLK + HALF + BLK


def pack(keys, values, width):
    tail = keys[:, 128:width]
    folded = jnp.concatenate([tail[:HALF], tail[HALF:]], axis=1)
    return jnp.concatenate([keys[:, :128], folded, values], axis=0)


def unpack(block):
    folded = block[BLK : BLK + HALF]
    low = lax.broadcasted_iota(jnp.int32, folded.shape, 1) < 64
    zero = jnp.zeros_like(folded)
    tails = jnp.concatenate([jnp.where(low, folded, zero), jnp.where(low, zero, folded)], axis=0)
    return jnp.concatenate([block[:BLK], tails], axis=1), block[BLK + HALF :]


def flip(index, step, size):
    shared = 0
    bit = 1
    while bit < size:
        shared = shared + lax.rem(index // bit, 2) * (step // bit % 2) * bit
        bit *= 2
    return index + step - 2 * shared


def picks(read, owner, blocks, cap):
    low = owner * blocks
    found = [jnp.int32(-1)] * cap
    count = jnp.int32(0)
    for entry in range(SEL):
        block = read(entry)
        here = (block >= low) & (block < low + blocks)
        for slot in range(cap):
            found[slot] = jnp.where(here & (count == slot), block, found[slot])
        count = count + here.astype(jnp.int32)
    return found


def kernel(
    n,
    groups,
    cap,
    scale,
    own_smem,
    own_table,
    query_hbm,
    key_hbm,
    value_hbm,
    ckey_hbm,
    cvalue_hbm,
    hidden_hbm,
    gate_hbm,
    weight_hbm,
    out_ref,
    query_ref,
    key_ref,
    value_ref,
    ckey_ref,
    cvalue_ref,
    hidden_ref,
    gate_ref,
    packed,
    query_wide,
    tables,
    tables_smem,
    outgoing,
    incoming,
    coarse,
    keys_wide,
    values_wide,
    picked_top,
    picked_sum,
    picked_out,
    coarse_top,
    coarse_sum,
    coarse_out,
    attended,
    weights,
    partial,
    arrived,
    own_part,
    input_sem,
    weight_sem,
    local_sem,
    table_send,
    table_recv,
    slot_send,
    slot_recv,
    coarse_send,
    coarse_recv,
    pass_send,
    pass_recv,
    part_send,
    part_recv,
):
    me = lax.axis_index("seq")
    group = lax.axis_index("grp")
    core = lax.rem(me, 2)
    sibling = me + 1 - 2 * core
    heads, width, _ = query_ref.shape
    blocks = value_ref.shape[0]
    columns = out_ref.shape[1]
    context = blocks * BLK * n
    span = 2 * TILE

    barrier = pltpu.get_barrier_semaphore()

    def greet(step, carry):
        pl.semaphore_signal(
            barrier, inc=1, device_id={"seq": flip(me, step, n)}, device_id_type=MESH
        )
        return carry

    lax.fori_loop(1, n, greet, 0)
    for step in range(1, groups):
        pl.semaphore_signal(
            barrier, inc=1, device_id={"grp": flip(group, step, groups)}, device_id_type=MESH
        )

    loads = [
        pltpu.make_async_copy(source, target, input_sem.at[index])
        for index, (source, target) in enumerate(
            [
                (ckey_hbm, ckey_ref),
                (cvalue_hbm, cvalue_ref),
                (key_hbm, key_ref),
                (value_hbm, value_ref),
                (query_hbm, query_ref),
                (hidden_hbm, hidden_ref),
                (gate_hbm, gate_ref),
            ]
        )
    ]
    for load in loads:
        load.start()

    def weight_copy(step):
        target = flip(group, step, groups)
        return pltpu.make_async_copy(
            weight_hbm.at[:, pl.ds(pl.multiple_of(target * columns, 128), columns)],
            weights.at[step],
            weight_sem.at[step],
        )

    for step in reversed(range(groups)):
        weight_copy(step).start()

    loads[0].wait()
    loads[1].wait()
    coarse[me] = pack(ckey_ref[...], cvalue_ref[...], width)
    loads[2].wait()
    loads[3].wait()
    for pair in range(blocks // 2):
        both = key_ref[:, pair * 128 : (pair + 1) * 128].T
        packed[2 * pair] = pack(both[:BLK], value_ref[2 * pair], width)
        packed[2 * pair + 1] = pack(both[BLK:], value_ref[2 * pair + 1], width)
    pl.semaphore_wait(barrier, n - 1 + groups - 1)

    def table_copy(step):
        return pltpu.make_async_remote_copy(
            src_ref=own_table,
            dst_ref=tables.at[step],
            send_sem=table_send.at[step],
            recv_sem=table_recv.at[step],
            device_id={"seq": flip(me, step, n)},
            device_id_type=MESH,
        )

    def coarse_copy(step):
        return pltpu.make_async_remote_copy(
            src_ref=coarse.at[me],
            dst_ref=coarse.at[me],
            send_sem=coarse_send.at[step],
            recv_sem=coarse_recv.at[step],
            device_id={"seq": flip(me, 2 * step, n)},
            device_id_type=MESH,
        )

    def pass_copy(step):
        origin = flip(me, 2 * step, n)
        return pltpu.make_async_remote_copy(
            src_ref=coarse.at[origin],
            dst_ref=coarse.at[origin],
            send_sem=pass_send.at[step],
            recv_sem=pass_recv.at[step],
            device_id={"seq": sibling},
            device_id_type=MESH,
        )

    def slot_copy(step):
        return pltpu.make_async_remote_copy(
            src_ref=outgoing.at[step],
            dst_ref=incoming.at[step],
            send_sem=slot_send.at[step],
            recv_sem=slot_recv.at[step],
            device_id={"seq": flip(me, step, n)},
            device_id_type=MESH,
        )

    def send_table(step, carry):
        table_copy(step).start()
        return carry

    lax.fori_loop(1, n, send_table, 0)

    def send_coarse(step, carry):
        coarse_copy(step).start()
        return carry

    lax.fori_loop(1, n // 2, send_coarse, 0)
    pass_copy(0).start()

    def wait_table(step, carry):
        table_copy(step).wait_recv()
        return carry

    lax.fori_loop(1, n, wait_table, 0)
    to_smem = pltpu.make_async_copy(tables, tables_smem, local_sem)
    to_smem.start()
    to_smem.wait()

    def send_slots(step, carry):
        wanted = picks(lambda entry: tables_smem[step, 0, 0, entry], me, blocks, cap)
        for slot in range(cap):
            outgoing[step, slot] = packed[jnp.maximum(wanted[slot] - me * blocks, 0)]
        slot_copy(step).start()
        return carry

    lax.fori_loop(1, n, send_slots, 0)

    loads[4].wait()
    for head in range(heads):
        one = query_ref[head]
        query_wide[:width, head * 128 : (head + 1) * 128] = one
        query_wide[width:, head * 128 : (head + 1) * 128] = one[128:]

    first_pos = context - TILE * n + me * TILE
    row = lax.broadcasted_iota(jnp.int32, (BLK, span), 0)
    query = lax.rem(lax.broadcasted_iota(jnp.int32, (BLK, span), 1), TILE)

    def fill(place, block):
        keys, values = unpack(block)
        keys_wide[place * BLK : (place + 1) * BLK] = keys
        return values

    def attend(count, bounds, stride, top_ref, sum_ref, out, first):
        lag = row * stride - query

        def chunk(index, carry):
            here = pl.ds(pl.multiple_of(index * span, span), span)
            scores = jnp.dot(
                keys_wide[: count * BLK], query_wide[:, here], preferred_element_type=jnp.float32
            )
            scores = jnp.concatenate(
                [
                    jnp.where(lag <= bounds[block], scores[block * BLK : (block + 1) * BLK], -jnp.inf)
                    for block in range(count)
                ],
                axis=0,
            )
            top = jnp.max(scores, axis=0, keepdims=True)
            if first:
                new = jnp.maximum(top, NEGATIVE)
            else:
                old = top_ref[:, here]
                new = jnp.maximum(old, top)
                factor = jnp.exp2((old - new) * scale)
            exponents = jnp.exp2((scores - new) * scale).astype(jnp.bfloat16)
            added = jnp.dot(
                values_wide[:, : count * BLK], exponents, preferred_element_type=jnp.float32
            )
            if first:
                out[:, here] = added[:128]
                sum_ref[:, here] = added[128:129]
            else:
                out[:, here] = out[:, here] * factor + added[:128]
                sum_ref[:, here] = sum_ref[:, here] * factor + added[128:129]
            top_ref[:, here] = new
            return carry

        lax.fori_loop(0, heads * TILE // span, chunk, 0, unroll=8)

    values_wide[128:, :] = jnp.ones_like(values_wide[128:, :])

    def attend_picked(owner, group_of, first):
        wanted = picks(lambda entry: own_smem[0, 0, entry], owner, blocks, cap)
        values = [fill(slot, group_of[slot]) for slot in range(cap)]
        values_wide[:128, : cap * BLK] = jnp.concatenate(values, axis=0).T
        bounds = [
            jnp.where(wanted[slot] < 0, -FAR, first_pos - wanted[slot] * BLK) for slot in range(cap)
        ]
        attend(cap, bounds, 1, picked_top, picked_sum, picked_out, first)

    mine = picks(lambda entry: own_smem[0, 0, entry], me, blocks, cap)
    attend_picked(me, [packed[jnp.maximum(block - me * blocks, 0)] for block in mine], True)

    loads[5].wait()
    loads[6].wait()
    gates = jax.nn.sigmoid(
        lax.dot_general(
            gate_ref[...],
            hidden_ref[...],
            (((1,), (1,)), ((), ())),
            preferred_element_type=jnp.float32,
        )
    )

    def forward(step, carry):
        coarse_copy(step).wait_recv()
        pass_copy(step).start()
        return carry

    lax.fori_loop(1, n // 2, forward, 0)

    def passed(step, carry):
        pass_copy(step).wait_recv()
        return carry

    lax.fori_loop(0, n // 2, passed, 0)

    pieces = min(n, 8)

    def coarse_step(index, first):
        values = [fill(piece, coarse[index * pieces + piece]) for piece in range(pieces)]
        values_wide[:128, : pieces * BLK] = jnp.concatenate(values, axis=0).T
        start = first_pos - (CLEN - 1) - index * (pieces * BLK * CSTRIDE)
        bounds = [start - piece * (BLK * CSTRIDE) for piece in range(pieces)]
        attend(pieces, bounds, CSTRIDE, coarse_top, coarse_sum, coarse_out, first)

    coarse_step(0, True)
    if n > pieces:

        def coarse_more(index, carry):
            coarse_step(index, False)
            return carry

        lax.fori_loop(1, n // pieces, coarse_more, 0)

    def picked_step(step, carry):
        slot_copy(step).wait_recv()
        owner = flip(me, step, n)
        attend_picked(owner, [incoming[step, slot] for slot in range(cap)], False)
        return carry

    lax.fori_loop(1, n, picked_step, 0)

    for head in range(heads):
        here = slice(head * 128, (head + 1) * 128)
        of_coarse = gates[head : head + 1] / coarse_sum[:, here]
        of_picked = gates[heads + head : heads + head + 1] / picked_sum[:, here]
        mixed = coarse_out[:, here] * of_coarse + picked_out[:, here] * of_picked
        attended[:, here] = mixed.T.astype(jnp.bfloat16)

    def part_copy(step):
        return pltpu.make_async_remote_copy(
            src_ref=partial.at[step],
            dst_ref=arrived.at[step],
            send_sem=part_send.at[step],
            recv_sem=part_recv.at[step],
            device_id={"grp": flip(group, step, groups)},
            device_id_type=MESH,
        )

    for step in reversed(range(1, groups)):
        weight_copy(step).wait()
        partial[step] = jnp.dot(
            attended[...], weights[step], preferred_element_type=jnp.float32
        ).astype(jnp.bfloat16)
        part_copy(step).start()
    weight_copy(0).wait()
    own_part[...] = jnp.dot(attended[...], weights[0], preferred_element_type=jnp.float32)

    def sent(step, carry):
        table_copy(step).wait_send()
        slot_copy(step).wait_send()
        return carry

    lax.fori_loop(1, n, sent, 0)

    def sent_coarse(step, carry):
        coarse_copy(step).wait_send()
        pass_copy(step).wait_send()
        return carry

    lax.fori_loop(1, n // 2, sent_coarse, 0)
    pass_copy(0).wait_send()
    total = own_part[...]
    for step in range(1, groups):
        part_copy(step).wait_recv()
        total = total + arrived[step].astype(jnp.float32)
    out_ref[...] = total.astype(out_ref.dtype)
    for step in range(1, groups):
        part_copy(step).wait_send()


def shards(
    queries,
    key_cache,
    group_value_cache,
    coarse_keys,
    coarse_values,
    hidden,
    gate_weight,
    out_weight,
    selected,
):
    n = lax.axis_size("seq")
    groups = lax.axis_size("grp")
    ctx_dev = key_cache.shape[1]
    heads = queries.shape[1]
    width = queries.shape[2]
    vwidth = group_value_cache.shape[2]
    rows = TILE * heads
    blocks = ctx_dev // BLK
    cap = max(1, 2 * SEL // n)
    columns = out_weight.shape[1] // groups
    pieces = min(n, 8)
    wide = max(pieces, cap) * BLK

    vmem = pl.BlockSpec(memory_space=pltpu.VMEM)
    hbm = pl.BlockSpec(memory_space=pl.ANY)
    dma = pltpu.SemaphoreType.DMA
    bf16, f32 = jnp.bfloat16, jnp.float32
    inputs = (
        queries.transpose(1, 2, 0),
        key_cache[0].T,
        group_value_cache.reshape(blocks, BLK, vwidth),
        coarse_keys[0],
        coarse_values[0],
        hidden,
        gate_weight[0].T,
    )
    return pl.pallas_call(
        functools.partial(kernel, n, groups, cap, width**-0.5 * math.log2(math.e)),
        out_shape=jax.ShapeDtypeStruct((TILE, columns), bf16),
        in_specs=[pl.BlockSpec(memory_space=pltpu.SMEM), vmem] + [hbm] * (len(inputs) + 1),
        out_specs=vmem,
        scratch_shapes=[pltpu.VMEM(one.shape, bf16) for one in inputs]
        + [
            pltpu.VMEM((blocks, UNIT, 128), bf16),
            pltpu.VMEM((256, rows), bf16),
            pltpu.VMEM((n, 1, 1, SEL), jnp.int32),
            pltpu.SMEM((n, 1, 1, SEL), jnp.int32),
            pltpu.VMEM((n, cap, UNIT, 128), bf16),
            pltpu.VMEM((n, cap, UNIT, 128), bf16),
            pltpu.VMEM((n, UNIT, 128), bf16),
            pltpu.VMEM((wide, 256), bf16),
            pltpu.VMEM((144, wide), bf16),
            pltpu.VMEM((1, rows), f32),
            pltpu.VMEM((1, rows), f32),
            pltpu.VMEM((vwidth, rows), f32),
            pltpu.VMEM((1, rows), f32),
            pltpu.VMEM((1, rows), f32),
            pltpu.VMEM((vwidth, rows), f32),
            pltpu.VMEM((TILE, heads * vwidth), bf16),
            pltpu.VMEM((groups, heads * vwidth, columns), bf16),
            pltpu.VMEM((groups, TILE, columns), bf16),
            pltpu.VMEM((groups, TILE, columns), bf16),
            pltpu.VMEM((TILE, columns), f32),
            dma((len(inputs),)),
            dma((groups,)),
            dma,
            dma((n,)),
            dma((n,)),
            dma((n,)),
            dma((n,)),
            dma((n // 2,)),
            dma((n // 2,)),
            dma((n // 2,)),
            dma((n // 2,)),
            dma((groups,)),
            dma((groups,)),
        ],
        compiler_params=pltpu.CompilerParams(
            collective_id=0, has_side_effects=True, vmem_limit_bytes=60 * 1024 * 1024
        ),
    )(selected, selected, *inputs, out_weight)


def solution(mesh):
    return jax.shard_map(
        shards,
        mesh=mesh,
        in_specs=(
            P("seq", "grp", None),
            P("grp", "seq", None),
            P("grp", "seq", None),
            P("grp", "seq", None),
            P("grp", "seq", None),
            P("seq", None),
            P("grp", None, None),
            P("grp", None),
            P("grp", "seq", None),
        ),
        out_specs=P("seq", "grp"),
        check_vma=False,
    )
```

profile of v0, /device:TPU:8, one launch (start us, length us, event | category | flops | bytes accessed | tf_op | source)
XLA Modules:
  0.0 54.2 jit_solution(9984321401418810850)
XLA Ops:
  0.0 52.6 %shard_map.91 = bf16[128,640]{1,0:T(8,128)(2,1)} custom-call(s32[1,1,16]{2,1,0:T(1,128)} %own_table.1, s32[1,1,16]{2,1,0:T(1,128)} %own_table.1, bf16[16,192,128]{2,1,0:T(8,128)(2,1)} %bitcast.10, bf16[192,1024]{1,0:T(8,128)(2,1)} %bitcast.11, bf16[16,64,128]{2,1,0:T(8,128)(2,1)} %bitcast.12, bf16[64,192]{1,0:T(8,128)(2,1)} %bitcast.14, ...), custom_call_target="tpu_custom_call" | custom-call | tf_op jit(solution)/shard_map/pallas_call | solution.py:454
  52.6 1.6 %copy.11 = bf16[128,640]{1,0:T(8,128)(2,1)} copy(bf16[128,640]{1,0:T(8,128)(2,1)} %shard_map.91) | data formatting | bytes 327680
where the time goes:
time: 54.4 us; the launch traced here: 54.2 us
  Pallas kernels  52.6 us (97%)
  local copies, waits for them, and re-layouts  1.6 us (3%)
    pallas_call x1, Pallas kernels, shards(): pl.pallas_call(functools.partial(kernel, n, groups, cap, width ** (-0.5)...  52.6 us
    unnamed x1, local copies, waits for them, and re-layouts  1.6 us

commit v1 on v0

--- a/solution.py
+++ b/solution.py
@@ -19,6 +19,7 @@
 MESH = pl.DeviceIdType.MESH
 HALF = BLK // 2
 UNIT = BLK + HALF + BLK
+MARK = 1 << 16
 
 
 def pack(keys, values, width):
@@ -35,13 +36,32 @@
     return jnp.concatenate([block[:BLK], tails], axis=1), block[BLK + HALF :]
 
 
+def bit_of(index, bit):
+    return index // bit % 2 if isinstance(index, int) else lax.rem(index // bit, 2)
+
+
 def flip(index, step, size):
     shared = 0
     bit = 1
     while bit < size:
-        shared = shared + lax.rem(index // bit, 2) * (step // bit % 2) * bit
+        shared = shared + bit_of(index, bit) * bit_of(step, bit) * bit
         bit *= 2
     return index + step - 2 * shared
+
+
+def exchanges(count):
+    found = []
+    p = 1
+    while p < count:
+        k = p
+        while k >= 1:
+            for j in range(k % p, count - k, 2 * k):
+                for i in range(min(k, count - j - k)):
+                    if (i + j) // (2 * p) == (i + j + k) // (2 * p):
+                        found.append((i + j, i + j + k))
+            k //= 2
+        p *= 2
+    return found
 
 
 def picks(read, owner, blocks, cap):
@@ -84,8 +104,10 @@
     query_wide,
     tables,
     tables_smem,
+    order_smem,
     outgoing,
-    incoming,
+    early,
+    late,
     coarse,
     keys_wide,
     values_wide,
@@ -123,6 +145,9 @@
     columns = out_ref.shape[1]
     context = blocks * BLK * n
     span = 2 * TILE
+    half = n // 2
+    near = half * cap
+    share = SEL // cap
 
     barrier = pltpu.get_barrier_semaphore()
 
@@ -208,12 +233,18 @@
             device_id_type=MESH,
         )
 
-    def slot_copy(step):
+    def slot_copy(step, slot, across):
+        if not across:
+            target = early.at[step * cap + slot]
+        elif slot == 0:
+            target = early.at[near + step - half]
+        else:
+            target = late[slot - 1].at[step - half]
         return pltpu.make_async_remote_copy(
-            src_ref=outgoing.at[step],
-            dst_ref=incoming.at[step],
-            send_sem=slot_send.at[step],
-            recv_sem=slot_recv.at[step],
+            src_ref=outgoing.at[step, slot],
+            dst_ref=target,
+            send_sem=slot_send.at[step, slot],
+            recv_sem=slot_recv.at[step, slot],
             device_id={"seq": flip(me, step, n)},
             device_id_type=MESH,
         )
@@ -240,14 +271,70 @@
     to_smem.start()
     to_smem.wait()
 
-    def send_slots(step, carry):
+    def fill_slots(step):
         wanted = picks(lambda entry: tables_smem[step, 0, 0, entry], me, blocks, cap)
         for slot in range(cap):
             outgoing[step, slot] = packed[jnp.maximum(wanted[slot] - me * blocks, 0)]
-        slot_copy(step).start()
-        return carry
-
-    lax.fori_loop(1, n, send_slots, 0)
+
+    def send_near(index, carry):
+        step = half - index
+        fill_slots(step)
+        for slot in range(cap):
+            slot_copy(step, slot, False).start()
+        return carry
+
+    side = me // half
+
+    def far_step(phase, index):
+        place = half - 2 - 2 * index + phase
+        return flip(me, half - side + (1 - 2 * side) * place, n)
+
+    def send_far(phase):
+        def fill_far(index, carry):
+            fill_slots(far_step(phase, index))
+            return carry
+
+        lax.fori_loop(0, half // 2, fill_far, 0)
+        for slot in range(cap):
+
+            def send_one(index, carry):
+                slot_copy(far_step(phase, index), slot, True).start()
+                return carry
+
+            lax.fori_loop(0, half // 2, send_one, 0)
+
+    lax.fori_loop(1, half - 1, send_near, 0)
+    send_far(0)
+    lax.fori_loop(half - 1, half, send_near, 0)
+    send_far(1)
+
+    def rank(step, carry):
+        near_one = step < half
+        owner = flip(me, step, n)
+        order_smem[0, owner] = jnp.where(near_one, step * cap, near + step - half)
+        order_smem[1, owner] = jnp.where(near_one, 1, half)
+        return carry
+
+    lax.fori_loop(0, n, rank, 0)
+    entries = [own_smem[0, 0, entry] for entry in range(SEL)]
+    owners = [entry // blocks for entry in entries]
+    marks = []
+    for entry in range(SEL):
+        slot = jnp.int32(0)
+        for other in range(entry):
+            slot = slot + (owners[other] == owners[entry]).astype(jnp.int32)
+        place = order_smem[0, owners[entry]] + order_smem[1, owners[entry]] * slot
+        marks.append(place * MARK + entries[entry])
+    for low, high in exchanges(SEL):
+        marks[low], marks[high] = (
+            jnp.minimum(marks[low], marks[high]),
+            jnp.maximum(marks[low], marks[high]),
+        )
+    for entry in range(SEL):
+        order_smem[2, entry] = marks[entry]
+    mine = picks(lambda entry: own_smem[0, 0, entry], me, blocks, cap)
+    for slot in range(cap):
+        early[slot] = packed[jnp.maximum(mine[slot] - me * blocks, 0)]
 
     loads[4].wait()
     for head in range(heads):
@@ -303,17 +390,23 @@
 
     values_wide[128:, :] = jnp.ones_like(values_wide[128:, :])
 
-    def attend_picked(owner, group_of, first):
-        wanted = picks(lambda entry: own_smem[0, 0, entry], owner, blocks, cap)
-        values = [fill(slot, group_of[slot]) for slot in range(cap)]
-        values_wide[:128, : cap * BLK] = jnp.concatenate(values, axis=0).T
-        bounds = [
-            jnp.where(wanted[slot] < 0, -FAR, first_pos - wanted[slot] * BLK) for slot in range(cap)
-        ]
-        attend(cap, bounds, 1, picked_top, picked_sum, picked_out, first)
-
-    mine = picks(lambda entry: own_smem[0, 0, entry], me, blocks, cap)
-    attend_picked(me, [packed[jnp.maximum(block - me * blocks, 0)] for block in mine], True)
+    def gather(mark, turn):
+        place = mark // MARK
+        block = early[jnp.minimum(place, near + half - 1)]
+        for slot in range(1, turn + 1):
+            start = near + slot * half
+            other = late[slot - 1][jnp.clip(place - start, 0, half - 1)]
+            block = jnp.where(place >= start, other, block)
+        return block
+
+    def attend_picked(turn):
+        count = min(share, 4)
+        for part in range(share // count):
+            marks = [order_smem[2, turn * share + part * count + index] for index in range(count)]
+            values = [fill(index, gather(mark, turn)) for index, mark in enumerate(marks)]
+            values_wide[:128, : count * BLK] = jnp.concatenate(values, axis=0).T
+            bounds = [first_pos - lax.rem(mark, MARK) * BLK for mark in marks]
+            attend(count, bounds, 1, picked_top, picked_sum, picked_out, turn + part == 0)
 
     loads[5].wait()
     loads[6].wait()
@@ -357,13 +450,20 @@
 
         lax.fori_loop(1, n // pieces, coarse_more, 0)
 
-    def picked_step(step, carry):
-        slot_copy(step).wait_recv()
-        owner = flip(me, step, n)
-        attend_picked(owner, [incoming[step, slot] for slot in range(cap)], False)
-        return carry
-
-    lax.fori_loop(1, n, picked_step, 0)
+    def wait_near(step, carry):
+        for slot in range(cap):
+            slot_copy(step, slot, False).wait_recv()
+        return carry
+
+    lax.fori_loop(1, half, wait_near, 0)
+    for turn in range(cap):
+
+        def wait_far(step, carry):
+            slot_copy(step, turn, True).wait_recv()
+            return carry
+
+        lax.fori_loop(half, n, wait_far, 0)
+        attend_picked(turn)
 
     for head in range(heads):
         here = slice(head * 128, (head + 1) * 128)
@@ -393,10 +493,20 @@
 
     def sent(step, carry):
         table_copy(step).wait_send()
-        slot_copy(step).wait_send()
         return carry
 
     lax.fori_loop(1, n, sent, 0)
+
+    def sent_slots(across):
+        def sent_one(step, carry):
+            for slot in range(cap):
+                slot_copy(step, slot, across).wait_send()
+            return carry
+
+        return sent_one
+
+    lax.fori_loop(1, half, sent_slots(False), 0)
+    lax.fori_loop(half, n, sent_slots(True), 0)
 
     def sent_coarse(step, carry):
         coarse_copy(step).wait_send()
@@ -436,7 +546,7 @@
     cap = max(1, 2 * SEL // n)
     columns = out_weight.shape[1] // groups
     pieces = min(n, 8)
-    wide = max(pieces, cap) * BLK
+    wide = max(pieces, 4) * BLK
 
     vmem = pl.BlockSpec(memory_space=pltpu.VMEM)
     hbm = pl.BlockSpec(memory_space=pl.ANY)
@@ -462,8 +572,10 @@
             pltpu.VMEM((256, rows), bf16),
             pltpu.VMEM((n, 1, 1, SEL), jnp.int32),
             pltpu.SMEM((n, 1, 1, SEL), jnp.int32),
+            pltpu.SMEM((3, max(n, SEL)), jnp.int32),
             pltpu.VMEM((n, cap, UNIT, 128), bf16),
-            pltpu.VMEM((n, cap, UNIT, 128), bf16),
+            pltpu.VMEM((n // 2 * (cap + 1), UNIT, 128), bf16),
+            [pltpu.VMEM((n // 2, UNIT, 128), bf16) for _ in range(cap - 1)],
             pltpu.VMEM((n, UNIT, 128), bf16),
             pltpu.VMEM((wide, 256), bf16),
             pltpu.VMEM((144, wide), bf16),
@@ -483,8 +595,8 @@
             dma,
             dma((n,)),
             dma((n,)),
-            dma((n,)),
-            dma((n,)),
+            dma((n, cap)),
+            dma((n, cap)),
             dma((n // 2,)),
             dma((n // 2,)),
             dma((n // 2,)),

time: 54.4 us -> 56.6 us (1.040)
  the two profiles are of different devices: /device:TPU:8 before, /device:TPU:0 now
where the time goes in v1:
time: 56.6 us; the launch traced here: 56.5 us
  Pallas kernels  54.8 us (97%)
  local copies, waits for them, and re-layouts  1.6 us (3%)
    pallas_call x1, Pallas kernels, shards(): pl.pallas_call(functools.partial(kernel, n, groups, cap, width ** (-0.5)...  54.8 us
    unnamed x1, local copies, waits for them, and re-layouts  1.6 us

profile of v1, /device:TPU:0, one launch (start us, length us, event | category | flops | bytes accessed | tf_op | source)
XLA Modules:
  0.0 56.5 jit_solution(4333133437073129018)
XLA Ops:
  0.0 54.8 %shard_map.91 = bf16[128,640]{1,0:T(8,128)(2,1)} custom-call(s32[1,1,16]{2,1,0:T(1,128)} %own_table.1, s32[1,1,16]{2,1,0:T(1,128)} %own_table.1, bf16[16,192,128]{2,1,0:T(8,128)(2,1)} %bitcast.10, bf16[192,1024]{1,0:T(8,128)(2,1)} %bitcast.11, bf16[16,64,128]{2,1,0:T(8,128)(2,1)} %bitcast.12, bf16[64,192]{1,0:T(8,128)(2,1)} %bitcast.14, ...), custom_call_target="tpu_custom_call" | custom-call | tf_op jit(solution)/shard_map/pallas_call | solution.py:564
  54.9 1.6 %copy.11 = bf16[128,640]{1,0:T(8,128)(2,1)} copy(bf16[128,640]{1,0:T(8,128)(2,1)} %shard_map.91) | data formatting | bytes 327680

commit v2 on v1

--- a/solution.py
+++ b/solution.py
@@ -20,6 +20,7 @@
 HALF = BLK // 2
 UNIT = BLK + HALF + BLK
 MARK = 1 << 16
+PART = SEL // 4
 
 
 def pack(keys, values, width):
@@ -146,8 +147,10 @@
     context = blocks * BLK * n
     span = 2 * TILE
     half = n // 2
-    near = half * cap
-    share = SEL // cap
+    chips = n // 2
+    ahead = n if cap == 1 else half + half // 2
+    ready = n if cap == 1 else ahead * cap
+    batch = half // 2 * (cap // 2)
 
     barrier = pltpu.get_barrier_semaphore()
 
@@ -212,34 +215,43 @@
             device_id_type=MESH,
         )
 
-    def coarse_copy(step):
+    def coarse_copy(held, bit):
+        unit = coarse.at[flip(me, 2 * held, n)]
         return pltpu.make_async_remote_copy(
-            src_ref=coarse.at[me],
-            dst_ref=coarse.at[me],
-            send_sem=coarse_send.at[step],
-            recv_sem=coarse_recv.at[step],
-            device_id={"seq": flip(me, 2 * step, n)},
+            src_ref=unit,
+            dst_ref=unit,
+            send_sem=coarse_send.at[held + bit],
+            recv_sem=coarse_recv.at[held + bit],
+            device_id={"seq": flip(me, 2 * bit, n)},
             device_id_type=MESH,
         )
 
+    def coarse_wait(held):
+        coarse_copy(0, held).wait_recv()
+
     def pass_copy(step):
-        origin = flip(me, 2 * step, n)
+        unit = coarse.at[flip(me, 2 * step, n)]
         return pltpu.make_async_remote_copy(
-            src_ref=coarse.at[origin],
-            dst_ref=coarse.at[origin],
+            src_ref=unit,
+            dst_ref=unit,
             send_sem=pass_send.at[step],
             recv_sem=pass_recv.at[step],
             device_id={"seq": sibling},
             device_id_type=MESH,
         )
 
-    def slot_copy(step, slot, across):
-        if not across:
-            target = early.at[step * cap + slot]
-        elif slot == 0:
-            target = early.at[near + step - half]
+    def bits_below(bit):
+        while bit > 1:
+            bit //= 2
+            yield bit
+
+    def slot_copy(step, slot, late_one):
+        if cap == 1:
+            target = early.at[step]
+        elif late_one:
+            target = late[slot // (cap // 2)].at[(step - half) * (cap // 2) + slot % (cap // 2)]
         else:
-            target = late[slot - 1].at[step - half]
+            target = early.at[(step - jnp.where(step < half, 0, half // 2)) * cap + slot]
         return pltpu.make_async_remote_copy(
             src_ref=outgoing.at[step, slot],
             dst_ref=target,
@@ -255,11 +267,8 @@
 
     lax.fori_loop(1, n, send_table, 0)
 
-    def send_coarse(step, carry):
-        coarse_copy(step).start()
-        return carry
-
-    lax.fori_loop(1, n // 2, send_coarse, 0)
+    for bit in bits_below(chips):
+        coarse_copy(0, bit).start()
     pass_copy(0).start()
 
     def wait_table(step, carry):
@@ -276,8 +285,7 @@
         for slot in range(cap):
             outgoing[step, slot] = packed[jnp.maximum(wanted[slot] - me * blocks, 0)]
 
-    def send_near(index, carry):
-        step = half - index
+    def send_near(step, carry):
         fill_slots(step)
         for slot in range(cap):
             slot_copy(step, slot, False).start()
@@ -285,34 +293,68 @@
 
     side = me // half
 
-    def far_step(phase, index):
-        place = half - 2 - 2 * index + phase
-        return flip(me, half - side + (1 - 2 * side) * place, n)
+    def far_step(phase, chip):
+        return flip(me, half - side + (1 - 2 * side) * (2 * chip + phase), n)
 
     def send_far(phase):
-        def fill_far(index, carry):
-            fill_slots(far_step(phase, index))
+        def fill_far(chip, carry):
+            fill_slots(far_step(phase, chip))
             return carry
 
         lax.fori_loop(0, half // 2, fill_far, 0)
-        for slot in range(cap):
-
-            def send_one(index, carry):
-                slot_copy(far_step(phase, index), slot, True).start()
+        if cap == 1:
+
+            def send_single(index, carry):
+                slot_copy(far_step(phase, half // 2 - 1 - index), 0, False).start()
                 return carry
 
-            lax.fori_loop(0, half // 2, send_one, 0)
-
-    lax.fori_loop(1, half - 1, send_near, 0)
+            lax.fori_loop(0, half // 2, send_single, 0)
+            return
+        lag = 2.5 if phase else -0.1
+        order = [
+            (slot + lag * (half // 2 - 1 - chip), chip, slot)
+            for chip in range(half // 2)
+            for slot in range(cap)
+        ]
+        for _, chip, slot in sorted(order):
+            step = far_step(phase, chip)
+
+            @pl.when(step < half + half // 2)
+            def _():
+                slot_copy(step, slot, True).start()
+
+            @pl.when(step >= half + half // 2)
+            def _():
+                slot_copy(step, slot, False).start()
+
     send_far(0)
-    lax.fori_loop(half - 1, half, send_near, 0)
+    for low in bits_below(chips):
+        for held in range(low, chips, 2 * low):
+            if low > 1:
+                coarse_wait(held)
+                for bit in bits_below(low):
+                    coarse_copy(held, bit).start()
+                pass_copy(held).start()
+    lax.fori_loop(2, half, send_near, 0)
+    lax.fori_loop(1, 2, send_near, 0)
     send_far(1)
+    for held in range(1, chips, 2):
+        coarse_wait(held)
+        pass_copy(held).start()
 
     def rank(step, carry):
-        near_one = step < half
         owner = flip(me, step, n)
-        order_smem[0, owner] = jnp.where(near_one, step * cap, near + step - half)
-        order_smem[1, owner] = jnp.where(near_one, 1, half)
+        if cap == 1:
+            order_smem[0, owner] = step
+            order_smem[1, owner] = 0
+        else:
+            last = (step >= half) & (step < half + half // 2)
+            order_smem[0, owner] = jnp.where(
+                last,
+                ready + (step - half) * (cap // 2),
+                (step - jnp.where(step < half, 0, half // 2)) * cap,
+            )
+            order_smem[1, owner] = jnp.where(last, batch - cap // 2, 0)
         return carry
 
     lax.fori_loop(0, n, rank, 0)
@@ -323,7 +365,8 @@
         slot = jnp.int32(0)
         for other in range(entry):
             slot = slot + (owners[other] == owners[entry]).astype(jnp.int32)
-        place = order_smem[0, owners[entry]] + order_smem[1, owners[entry]] * slot
+        place = order_smem[0, owners[entry]] + slot
+        place = place + jnp.where(slot >= cap // 2, order_smem[1, owners[entry]], 0)
         marks.append(place * MARK + entries[entry])
     for low, high in exchanges(SEL):
         marks[low], marks[high] = (
@@ -353,12 +396,16 @@
 
     def attend(count, bounds, stride, top_ref, sum_ref, out, first):
         lag = row * stride - query
-
-        def chunk(index, carry):
-            here = pl.ds(pl.multiple_of(index * span, span), span)
-            scores = jnp.dot(
+        total = heads * TILE // span
+
+        def score(index):
+            here = slice(index * span, (index + 1) * span)
+            return jnp.dot(
                 keys_wide[: count * BLK], query_wide[:, here], preferred_element_type=jnp.float32
             )
+
+        def soft(index, scores):
+            here = slice(index * span, (index + 1) * span)
             scores = jnp.concatenate(
                 [
                     jnp.where(lag <= bounds[block], scores[block * BLK : (block + 1) * BLK], -jnp.inf)
@@ -369,11 +416,16 @@
             top = jnp.max(scores, axis=0, keepdims=True)
             if first:
                 new = jnp.maximum(top, NEGATIVE)
+                factor = None
             else:
                 old = top_ref[:, here]
                 new = jnp.maximum(old, top)
                 factor = jnp.exp2((old - new) * scale)
-            exponents = jnp.exp2((scores - new) * scale).astype(jnp.bfloat16)
+            top_ref[:, here] = new
+            return jnp.exp2((scores - new) * scale).astype(jnp.bfloat16), factor
+
+        def value(index, exponents, factor):
+            here = slice(index * span, (index + 1) * span)
             added = jnp.dot(
                 values_wide[:, : count * BLK], exponents, preferred_element_type=jnp.float32
             )
@@ -383,30 +435,30 @@
             else:
                 out[:, here] = out[:, here] * factor + added[:128]
                 sum_ref[:, here] = sum_ref[:, here] * factor + added[128:129]
-            top_ref[:, here] = new
-            return carry
-
-        lax.fori_loop(0, heads * TILE // span, chunk, 0, unroll=8)
+
+        ready = score(0)
+        for index in range(total):
+            later = score(index + 1) if index + 1 < total else None
+            value(index, *soft(index, ready))
+            ready = later
 
     values_wide[128:, :] = jnp.ones_like(values_wide[128:, :])
 
     def gather(mark, turn):
         place = mark // MARK
-        block = early[jnp.minimum(place, near + half - 1)]
-        for slot in range(1, turn + 1):
-            start = near + slot * half
-            other = late[slot - 1][jnp.clip(place - start, 0, half - 1)]
+        block = early[jnp.minimum(place, ready - 1)]
+        for index in range(turn):
+            start = ready + index * batch
+            other = late[index][jnp.clip(place - start, 0, batch - 1)]
             block = jnp.where(place >= start, other, block)
         return block
 
-    def attend_picked(turn):
-        count = min(share, 4)
-        for part in range(share // count):
-            marks = [order_smem[2, turn * share + part * count + index] for index in range(count)]
-            values = [fill(index, gather(mark, turn)) for index, mark in enumerate(marks)]
-            values_wide[:128, : count * BLK] = jnp.concatenate(values, axis=0).T
-            bounds = [first_pos - lax.rem(mark, MARK) * BLK for mark in marks]
-            attend(count, bounds, 1, picked_top, picked_sum, picked_out, turn + part == 0)
+    def attend_picked(turn, start):
+        marks = [order_smem[2, start + index] for index in range(PART)]
+        values = [fill(index, gather(mark, turn)) for index, mark in enumerate(marks)]
+        values_wide[:128, : PART * BLK] = jnp.concatenate(values, axis=0).T
+        bounds = [first_pos - lax.rem(mark, MARK) * BLK for mark in marks]
+        attend(PART, bounds, 1, picked_top, picked_sum, picked_out, start == 0)
 
     loads[5].wait()
     loads[6].wait()
@@ -419,13 +471,6 @@
         )
     )
 
-    def forward(step, carry):
-        coarse_copy(step).wait_recv()
-        pass_copy(step).start()
-        return carry
-
-    lax.fori_loop(1, n // 2, forward, 0)
-
     def passed(step, carry):
         pass_copy(step).wait_recv()
         return carry
@@ -450,20 +495,26 @@
 
         lax.fori_loop(1, n // pieces, coarse_more, 0)
 
-    def wait_near(step, carry):
-        for slot in range(cap):
-            slot_copy(step, slot, False).wait_recv()
-        return carry
-
-    lax.fori_loop(1, half, wait_near, 0)
-    for turn in range(cap):
-
-        def wait_far(step, carry):
-            slot_copy(step, turn, True).wait_recv()
+    def wait_slots(start, stop, slots, late_one):
+        def wait_one(step, carry):
+            for slot in slots:
+                slot_copy(step, slot, late_one).wait_recv()
             return carry
 
-        lax.fori_loop(half, n, wait_far, 0)
-        attend_picked(turn)
+        lax.fori_loop(start, stop, wait_one, 0)
+
+    if cap == 1:
+        wait_slots(1, n, [0], False)
+        for start in range(0, SEL, PART):
+            attend_picked(0, start)
+    else:
+        wait_slots(1, half, range(cap), False)
+        wait_slots(half + half // 2, n, range(cap), False)
+        for start in range(0, SEL // 2, PART):
+            attend_picked(0, start)
+        for turn in range(2):
+            wait_slots(half, half + half // 2, range(turn * cap // 2, (turn + 1) * cap // 2), True)
+            attend_picked(turn + 1, SEL // 2 + turn * PART)
 
     for head in range(heads):
         here = slice(head * 128, (head + 1) * 128)
@@ -497,24 +548,16 @@
 
     lax.fori_loop(1, n, sent, 0)
 
-    def sent_slots(across):
-        def sent_one(step, carry):
-            for slot in range(cap):
-                slot_copy(step, slot, across).wait_send()
-            return carry
-
-        return sent_one
-
-    lax.fori_loop(1, half, sent_slots(False), 0)
-    lax.fori_loop(half, n, sent_slots(True), 0)
-
-    def sent_coarse(step, carry):
-        coarse_copy(step).wait_send()
-        pass_copy(step).wait_send()
-        return carry
-
-    lax.fori_loop(1, n // 2, sent_coarse, 0)
-    pass_copy(0).wait_send()
+    def sent_slots(step, carry):
+        for slot in range(cap):
+            slot_copy(step, slot, False).wait_send()
+        return carry
+
+    lax.fori_loop(1, n, sent_slots, 0)
+    for held in range(chips):
+        if held:
+            coarse_copy(0, held).wait_send()
+        pass_copy(held).wait_send()
     total = own_part[...]
     for step in range(1, groups):
         part_copy(step).wait_recv()
@@ -546,7 +589,7 @@
     cap = max(1, 2 * SEL // n)
     columns = out_weight.shape[1] // groups
     pieces = min(n, 8)
-    wide = max(pieces, 4) * BLK
+    wide = max(pieces, PART) * BLK
 
     vmem = pl.BlockSpec(memory_space=pltpu.VMEM)
     hbm = pl.BlockSpec(memory_space=pl.ANY)
@@ -563,7 +606,7 @@
     )
     return pl.pallas_call(
         functools.partial(kernel, n, groups, cap, width**-0.5 * math.log2(math.e)),
-        out_shape=jax.ShapeDtypeStruct((TILE, columns), bf16),
+        out_shape=pltpu.VMEM((TILE, columns), bf16),
         in_specs=[pl.BlockSpec(memory_space=pltpu.SMEM), vmem] + [hbm] * (len(inputs) + 1),
         out_specs=vmem,
         scratch_shapes=[pltpu.VMEM(one.shape, bf16) for one in inputs]
@@ -574,8 +617,8 @@
             pltpu.SMEM((n, 1, 1, SEL), jnp.int32),
             pltpu.SMEM((3, max(n, SEL)), jnp.int32),
             pltpu.VMEM((n, cap, UNIT, 128), bf16),
-            pltpu.VMEM((n // 2 * (cap + 1), UNIT, 128), bf16),
-            [pltpu.VMEM((n // 2, UNIT, 128), bf16) for _ in range(cap - 1)],
+            pltpu.VMEM((n if cap == 1 else n * cap * 3 // 4, UNIT, 128), bf16),
+            [pltpu.VMEM((n * cap // 8, UNIT, 128), bf16) for _ in range(2 if cap > 1 else 0)],
             pltpu.VMEM((n, UNIT, 128), bf16),
             pltpu.VMEM((wide, 256), bf16),
             pltpu.VMEM((144, wide), bf16),

time: 56.6 us -> 53.3 us (0.942)
  the two profiles are of different devices: /device:TPU:0 before, /device:TPU:8 now
where the time goes in v2:
time: 53.3 us; the launch traced here: 53.1 us
  Pallas kernels  52.4 us (98%)
  local copies, waits for them, and re-layouts  0.67 us (1%)
    pallas_call x1, Pallas kernels, shards(): pl.pallas_call(functools.partial(kernel, n, groups, cap, width ** (-0.5)...  52.4 us

profile of v2, /device:TPU:8, one launch (start us, length us, event | category | flops | bytes accessed | tf_op | source)
XLA Modules:
  0.0 53.1 jit_solution(11952224625364150439)
XLA Ops:
  0.0 52.4 %shard_map.91 = bf16[128,640]{1,0:T(8,128)(2,1)S(1)} custom-call(s32[1,1,16]{2,1,0:T(1,128)} %own_table.1, s32[1,1,16]{2,1,0:T(1,128)} %own_table.1, bf16[16,192,128]{2,1,0:T(8,128)(2,1)} %bitcast.10, bf16[192,1024]{1,0:T(8,128)(2,1)} %bitcast.11, bf16[16,64,128]{2,1,0:T(8,128)(2,1)} %bitcast.12, bf16[64,192]{1,0:T(8,128)(2,1)} %bitcast.14, ...), custom_call_target="tpu_custom_call" | custom-call | tf_op jit(solution)/shard_map/pallas_call | solution.py:607
  52.4 0.7 %copy.11 = bf16[128,640]{1,0:T(8,128)(2,1)} copy(bf16[128,640]{1,0:T(8,128)(2,1)S(1)} %shard_map.91) | data formatting | bytes 327680

commit v3 on v2

--- a/solution.py
+++ b/solution.py
@@ -103,7 +103,6 @@
     gate_ref,
     packed,
     query_wide,
-    tables,
     tables_smem,
     order_smem,
     outgoing,
@@ -125,7 +124,6 @@
     own_part,
     input_sem,
     weight_sem,
-    local_sem,
     table_send,
     table_recv,
     slot_send,
@@ -148,9 +146,11 @@
     span = 2 * TILE
     half = n // 2
     chips = n // 2
-    ahead = n if cap == 1 else half + half // 2
-    ready = n if cap == 1 else ahead * cap
-    batch = half // 2 * (cap // 2)
+    staged = len(late) == 2
+    ready = early.shape[0]
+    batch = ready // 6
+    side = me // half
+    outer = (me < half - 2) | (me >= half + 2)
 
     barrier = pltpu.get_barrier_semaphore()
 
@@ -208,7 +208,7 @@
     def table_copy(step):
         return pltpu.make_async_remote_copy(
             src_ref=own_table,
-            dst_ref=tables.at[step],
+            dst_ref=tables_smem.at[step],
             send_sem=table_send.at[step],
             recv_sem=table_recv.at[step],
             device_id={"seq": flip(me, step, n)},
@@ -246,12 +246,13 @@
             yield bit
 
     def slot_copy(step, slot, late_one):
-        if cap == 1:
-            target = early.at[step]
+        if not staged:
+            target = early.at[step * cap + slot]
         elif late_one:
-            target = late[slot // (cap // 2)].at[(step - half) * (cap // 2) + slot % (cap // 2)]
+            target = late[slot // 2].at[lax.rem(step, 2) * 2 + slot % 2]
         else:
-            target = early.at[(step - jnp.where(step < half, 0, half // 2)) * cap + slot]
+            place = jnp.where(step < half, step, half + lax.rem(step, 2))
+            target = early.at[place * cap + slot]
         return pltpu.make_async_remote_copy(
             src_ref=outgoing.at[step, slot],
             dst_ref=target,
@@ -271,16 +272,8 @@
         coarse_copy(0, bit).start()
     pass_copy(0).start()
 
-    def wait_table(step, carry):
+    def fill_slots(step):
         table_copy(step).wait_recv()
-        return carry
-
-    lax.fori_loop(1, n, wait_table, 0)
-    to_smem = pltpu.make_async_copy(tables, tables_smem, local_sem)
-    to_smem.start()
-    to_smem.wait()
-
-    def fill_slots(step):
         wanted = picks(lambda entry: tables_smem[step, 0, 0, entry], me, blocks, cap)
         for slot in range(cap):
             outgoing[step, slot] = packed[jnp.maximum(wanted[slot] - me * blocks, 0)]
@@ -291,8 +284,6 @@
             slot_copy(step, slot, False).start()
         return carry
 
-    side = me // half
-
     def far_step(phase, chip):
         return flip(me, half - side + (1 - 2 * side) * (2 * chip + phase), n)
 
@@ -302,15 +293,17 @@
             return carry
 
         lax.fori_loop(0, half // 2, fill_far, 0)
-        if cap == 1:
+        if not staged:
 
             def send_single(index, carry):
-                slot_copy(far_step(phase, half // 2 - 1 - index), 0, False).start()
+                step = far_step(phase, half // 2 - 1 - index)
+                for slot in range(cap):
+                    slot_copy(step, slot, False).start()
                 return carry
 
             lax.fori_loop(0, half // 2, send_single, 0)
             return
-        lag = 2.5 if phase else -0.1
+        lag = 1.5 if phase else -0.1
         order = [
             (slot + lag * (half // 2 - 1 - chip), chip, slot)
             for chip in range(half // 2)
@@ -319,15 +312,25 @@
         for _, chip, slot in sorted(order):
             step = far_step(phase, chip)
 
-            @pl.when(step < half + half // 2)
+            @pl.when(outer)
+            def _():
+                slot_copy(step, slot, False).start()
+
+            @pl.when(jnp.logical_not(outer))
             def _():
                 slot_copy(step, slot, True).start()
 
-            @pl.when(step >= half + half // 2)
-            def _():
-                slot_copy(step, slot, False).start()
-
-    send_far(0)
+    def send_chip(start, stop):
+        lax.fori_loop(start, stop, send_near, 0)
+
+    @pl.when(outer)
+    def _():
+        send_chip(2, half)
+
+    @pl.when(jnp.logical_not(outer))
+    def _():
+        send_far(0)
+
     for low in bits_below(chips):
         for held in range(low, chips, 2 * low):
             if low > 1:
@@ -335,8 +338,16 @@
                 for bit in bits_below(low):
                     coarse_copy(held, bit).start()
                 pass_copy(held).start()
-    lax.fori_loop(2, half, send_near, 0)
-    lax.fori_loop(1, 2, send_near, 0)
+
+    @pl.when(outer)
+    def _():
+        send_far(0)
+
+    @pl.when(jnp.logical_not(outer))
+    def _():
+        send_chip(2, half)
+
+    send_chip(1, 2)
     send_far(1)
     for held in range(1, chips, 2):
         coarse_wait(held)
@@ -344,17 +355,15 @@
 
     def rank(step, carry):
         owner = flip(me, step, n)
-        if cap == 1:
-            order_smem[0, owner] = step
+        if not staged:
+            order_smem[0, owner] = step * cap
             order_smem[1, owner] = 0
         else:
-            last = (step >= half) & (step < half + half // 2)
-            order_smem[0, owner] = jnp.where(
-                last,
-                ready + (step - half) * (cap // 2),
-                (step - jnp.where(step < half, 0, half // 2)) * cap,
-            )
-            order_smem[1, owner] = jnp.where(last, batch - cap // 2, 0)
+            inner = (owner >= half - 2) & (owner < half + 2)
+            last = (step >= half) & inner
+            place = jnp.where(step < half, step, half + lax.rem(step, 2))
+            order_smem[0, owner] = jnp.where(last, ready + lax.rem(step, 2) * 2, place * cap)
+            order_smem[1, owner] = jnp.where(last, batch - 2, 0)
         return carry
 
     lax.fori_loop(0, n, rank, 0)
@@ -366,7 +375,7 @@
         for other in range(entry):
             slot = slot + (owners[other] == owners[entry]).astype(jnp.int32)
         place = order_smem[0, owners[entry]] + slot
-        place = place + jnp.where(slot >= cap // 2, order_smem[1, owners[entry]], 0)
+        place = place + jnp.where(slot >= 2, order_smem[1, owners[entry]], 0)
         marks.append(place * MARK + entries[entry])
     for low, high in exchanges(SEL):
         marks[low], marks[high] = (
@@ -495,25 +504,26 @@
 
         lax.fori_loop(1, n // pieces, coarse_more, 0)
 
-    def wait_slots(start, stop, slots, late_one):
-        def wait_one(step, carry):
+    def wait_slots(start, stop, slots, late_one, base=None):
+        def wait_one(index, carry):
+            step = index if base is None else flip(me, base + index, n)
             for slot in slots:
                 slot_copy(step, slot, late_one).wait_recv()
             return carry
 
         lax.fori_loop(start, stop, wait_one, 0)
 
-    if cap == 1:
-        wait_slots(1, n, [0], False)
+    if not staged:
+        wait_slots(1, n, range(cap), False)
         for start in range(0, SEL, PART):
             attend_picked(0, start)
     else:
         wait_slots(1, half, range(cap), False)
-        wait_slots(half + half // 2, n, range(cap), False)
+        wait_slots(0, 2, range(cap), False, (n - 2) * (1 - side))
         for start in range(0, SEL // 2, PART):
             attend_picked(0, start)
         for turn in range(2):
-            wait_slots(half, half + half // 2, range(turn * cap // 2, (turn + 1) * cap // 2), True)
+            wait_slots(0, 2, range(turn * 2, turn * 2 + 2), True, half - 2 * side)
             attend_picked(turn + 1, SEL // 2 + turn * PART)
 
     for head in range(heads):
@@ -590,6 +600,7 @@
     columns = out_weight.shape[1] // groups
     pieces = min(n, 8)
     wide = max(pieces, PART) * BLK
+    staged = n == 8 and cap == 4
 
     vmem = pl.BlockSpec(memory_space=pltpu.VMEM)
     hbm = pl.BlockSpec(memory_space=pl.ANY)
@@ -613,12 +624,11 @@
         + [
             pltpu.VMEM((blocks, UNIT, 128), bf16),
             pltpu.VMEM((256, rows), bf16),
-            pltpu.VMEM((n, 1, 1, SEL), jnp.int32),
             pltpu.SMEM((n, 1, 1, SEL), jnp.int32),
             pltpu.SMEM((3, max(n, SEL)), jnp.int32),
             pltpu.VMEM((n, cap, UNIT, 128), bf16),
-            pltpu.VMEM((n if cap == 1 else n * cap * 3 // 4, UNIT, 128), bf16),
-            [pltpu.VMEM((n * cap // 8, UNIT, 128), bf16) for _ in range(2 if cap > 1 else 0)],
+            pltpu.VMEM(((n - 2 * staged) * cap, UNIT, 128), bf16),
+            [pltpu.VMEM((cap, UNIT, 128), bf16) for _ in range(2 * staged)],
             pltpu.VMEM((n, UNIT, 128), bf16),
             pltpu.VMEM((wide, 256), bf16),
             pltpu.VMEM((144, wide), bf16),
@@ -635,7 +645,6 @@
             pltpu.VMEM((TILE, columns), f32),
             dma((len(inputs),)),
             dma((groups,)),
-            dma,
             dma((n,)),
             dma((n,)),
             dma((n, cap)),

time: 53.3 us -> 49.1 us (0.921)
  the two profiles are of different devices: /device:TPU:8 before, /device:TPU:0 now
where the time goes in v3:
time: 49.1 us; the launch traced here: 49 us
  Pallas kernels  48.3 us (98%)
  local copies, waits for them, and re-layouts  0.67 us (1%)
    pallas_call x1, Pallas kernels, shards(): pl.pallas_call(functools.partial(kernel, n, groups, cap, width ** (-0.5)...  48.3 us

profile of v3, /device:TPU:0, one launch (start us, length us, event | category | flops | bytes accessed | tf_op | source)
XLA Modules:
  0.0 49.0 jit_solution(15071178641864065179)
XLA Ops:
  0.0 48.3 %shard_map.91 = bf16[128,640]{1,0:T(8,128)(2,1)S(1)} custom-call(s32[1,1,16]{2,1,0:T(1,128)} %own_table.1, s32[1,1,16]{2,1,0:T(1,128)} %own_table.1, bf16[16,192,128]{2,1,0:T(8,128)(2,1)} %bitcast.10, bf16[192,1024]{1,0:T(8,128)(2,1)} %bitcast.11, bf16[16,64,128]{2,1,0:T(8,128)(2,1)} %bitcast.12, bf16[64,192]{1,0:T(8,128)(2,1)} %bitcast.14, ...), custom_call_target="tpu_custom_call" | custom-call | tf_op jit(solution)/shard_map/pallas_call | solution.py:618
  48.3 0.7 %copy.11 = bf16[128,640]{1,0:T(8,128)(2,1)} copy(bf16[128,640]{1,0:T(8,128)(2,1)S(1)} %shard_map.91) | data formatting | bytes 327680

commit v4 on v3

--- a/solution.py
+++ b/solution.py
@@ -134,6 +134,7 @@
     pass_recv,
     part_send,
     part_recv,
+    hello,
 ):
     me = lax.axis_index("seq")
     group = lax.axis_index("grp")
@@ -160,7 +161,14 @@
         )
         return carry
 
-    lax.fori_loop(1, n, greet, 0)
+    inner = jnp.logical_not(outer)
+    lax.fori_loop(1, half if staged else n, greet, 0)
+    if staged:
+
+        @pl.when(inner)
+        def _():
+            lax.fori_loop(n - 2, n, greet, 0)
+
     for step in range(1, groups):
         pl.semaphore_signal(
             barrier, inc=1, device_id={"grp": flip(group, step, groups)}, device_id_type=MESH
@@ -203,7 +211,23 @@
         both = key_ref[:, pair * 128 : (pair + 1) * 128].T
         packed[2 * pair] = pack(both[:BLK], value_ref[2 * pair], width)
         packed[2 * pair + 1] = pack(both[BLK:], value_ref[2 * pair + 1], width)
-    pl.semaphore_wait(barrier, n - 1 + groups - 1)
+    if not staged:
+        pl.semaphore_wait(barrier, n - 1 + groups - 1)
+    else:
+
+        @pl.when(inner)
+        def _():
+            pl.semaphore_wait(barrier, half + 1 + groups - 1)
+
+        @pl.when(outer)
+        def _():
+            pl.semaphore_wait(barrier, half - 1 + groups - 1)
+
+    def say(kind, step):
+        pl.semaphore_signal(
+            hello.at[kind], inc=1, device_id={"seq": flip(me, step, n)}, device_id_type=MESH
+        )
+
 
     def table_copy(step):
         return pltpu.make_async_remote_copy(
@@ -215,16 +239,26 @@
             device_id_type=MESH,
         )
 
-    def coarse_copy(held, bit):
+    def coarse_copy(held, bit, index=None):
         unit = coarse.at[flip(me, 2 * held, n)]
+        landing = flip(held, bit, chips)
         return pltpu.make_async_remote_copy(
             src_ref=unit,
             dst_ref=unit,
-            send_sem=coarse_send.at[held + bit],
-            recv_sem=coarse_recv.at[held + bit],
+            send_sem=coarse_send.at[landing if index is None else index],
+            recv_sem=coarse_recv.at[landing],
             device_id={"seq": flip(me, 2 * bit, n)},
             device_id_type=MESH,
         )
+
+    hops = [(0, 3), (0, 1), (1, 3), (3, 1), (2, 1)]
+
+    def hop(index):
+        return coarse_copy(*hops[index], index)
+
+    def coarse_pass(held):
+        coarse_wait(held)
+        pass_copy(held).start()
 
     def coarse_wait(held):
         coarse_copy(0, held).wait_recv()
@@ -266,10 +300,21 @@
         table_copy(step).start()
         return carry
 
-    lax.fori_loop(1, n, send_table, 0)
-
-    for bit in bits_below(chips):
-        coarse_copy(0, bit).start()
+    lax.fori_loop(1, half if staged else n, send_table, 0)
+
+    if staged:
+
+        @pl.when(inner)
+        def _():
+            say(0, n - 2)
+            say(0, 2)
+            lax.fori_loop(n - 2, n, send_table, 0)
+            hop(0).start()
+
+        hop(1).start()
+    else:
+        for bit in bits_below(chips):
+            coarse_copy(0, bit).start()
     pass_copy(0).start()
 
     def fill_slots(step):
@@ -287,12 +332,12 @@
     def far_step(phase, chip):
         return flip(me, half - side + (1 - 2 * side) * (2 * chip + phase), n)
 
-    def send_far(phase):
+    def send_far(phase, first, last):
         def fill_far(chip, carry):
             fill_slots(far_step(phase, chip))
             return carry
 
-        lax.fori_loop(0, half // 2, fill_far, 0)
+        lax.fori_loop(first, last, fill_far, 0)
         if not staged:
 
             def send_single(index, carry):
@@ -306,7 +351,7 @@
         lag = 1.5 if phase else -0.1
         order = [
             (slot + lag * (half // 2 - 1 - chip), chip, slot)
-            for chip in range(half // 2)
+            for chip in range(first, last)
             for slot in range(cap)
         ]
         for _, chip, slot in sorted(order):
@@ -316,42 +361,66 @@
             def _():
                 slot_copy(step, slot, False).start()
 
-            @pl.when(jnp.logical_not(outer))
+            @pl.when(inner)
             def _():
                 slot_copy(step, slot, True).start()
 
     def send_chip(start, stop):
         lax.fori_loop(start, stop, send_near, 0)
 
-    @pl.when(outer)
-    def _():
-        send_chip(2, half)
-
-    @pl.when(jnp.logical_not(outer))
-    def _():
-        send_far(0)
-
-    for low in bits_below(chips):
-        for held in range(low, chips, 2 * low):
-            if low > 1:
-                coarse_wait(held)
-                for bit in bits_below(low):
-                    coarse_copy(held, bit).start()
-                pass_copy(held).start()
-
-    @pl.when(outer)
-    def _():
-        send_far(0)
-
-    @pl.when(jnp.logical_not(outer))
-    def _():
-        send_chip(2, half)
-
-    send_chip(1, 2)
-    send_far(1)
-    for held in range(1, chips, 2):
-        coarse_wait(held)
-        pass_copy(held).start()
+    if staged:
+
+        @pl.when(inner)
+        def _():
+            @pl.when(side == 0)
+            def _():
+                send_chip(2, half)
+
+            send_far(0, 0, 1)
+            pl.semaphore_wait(hello.at[0], 1)
+            say(1, 2)
+            lax.fori_loop(half, n - 2, send_table, 0)
+
+            @pl.when(side == 1)
+            def _():
+                send_chip(2, half)
+
+            coarse_pass(3)
+            hop(3).start()
+            coarse_pass(1)
+            hop(2).start()
+            send_far(0, 1, 2)
+            coarse_pass(2)
+            hop(4).start()
+
+        @pl.when(outer)
+        def _():
+            pl.semaphore_wait(hello.at[0], 1)
+            lax.fori_loop(half, n - 2, send_table, 0)
+            pl.semaphore_wait(hello.at[1], 1)
+            lax.fori_loop(n - 2, n, send_table, 0)
+            send_chip(2, half)
+            send_far(0, 0, 2)
+
+        send_chip(1, 2)
+        send_far(1, 0, 2)
+
+        @pl.when(outer)
+        def _():
+            for held in (1, 2, 3):
+                coarse_pass(held)
+    else:
+        for low in bits_below(chips):
+            for held in range(low, chips, 2 * low):
+                if low > 1:
+                    coarse_pass(held)
+                    for bit in bits_below(low):
+                        coarse_copy(held, bit).start()
+        send_chip(1, half)
+        send_far(0, 0, half // 2)
+        send_far(1, 0, half // 2)
+        for held in range(1, chips, 2):
+            coarse_pass(held)
 
     def rank(step, carry):
         owner = flip(me, step, n)
@@ -565,9 +634,17 @@
 
     lax.fori_loop(1, n, sent_slots, 0)
     for held in range(chips):
-        if held:
+        if held and not staged:
             coarse_copy(0, held).wait_send()
         pass_copy(held).wait_send()
+    if staged:
+        hop(1).wait_send()
+
+        @pl.when(inner)
+        def _():
+            for index in (0, 2, 3, 4):
+                hop(index).wait_send()
+
     total = own_part[...]
     for step in range(1, groups):
         part_copy(step).wait_recv()
@@ -649,12 +726,13 @@
             dma((n,)),
             dma((n, cap)),
             dma((n, cap)),
-            dma((n // 2,)),
+            dma((n // 2 + 1,)),
             dma((n // 2,)),
             dma((n // 2,)),
             dma((n // 2,)),
             dma((groups,)),
             dma((groups,)),
+            pltpu.SemaphoreType.REGULAR((2,)),
         ],
         compiler_params=pltpu.CompilerParams(
             collective_id=0, has_side_effects=True, vmem_limit_bytes=60 * 1024 * 1024

time: 49.1 us -> 48 us (0.978)
  Pallas kernels: 48.3 us -> 47.2 us
    pallas_call x1, Pallas kernels: 48.3 us -> 47.2 us  [shards(): pl.pallas_call(functools.partial(kernel, n, groups, cap, width ** (-0.5)...]
where the time goes in v4:
time: 48 us; the launch traced here: 47.9 us
  Pallas kernels  47.2 us (98%)
  local copies, waits for them, and re-layouts  0.67 us (1%)
    pallas_call x1, Pallas kernels, shards(): pl.pallas_call(functools.partial(kernel, n, groups, cap, width ** (-0.5)...  47.2 us

profile of v4, /device:TPU:0, one launch (start us, length us, event | category | flops | bytes accessed | tf_op | source)
XLA Modules:
  0.0 47.9 jit_solution(5725806342580720006)
XLA Ops:
  0.0 47.2 %shard_map.91 = bf16[128,640]{1,0:T(8,128)(2,1)S(1)} custom-call(s32[1,1,16]{2,1,0:T(1,128)} %own_table.1, s32[1,1,16]{2,1,0:T(1,128)} %own_table.1, bf16[16,192,128]{2,1,0:T(8,128)(2,1)} %bitcast.10, bf16[192,1024]{1,0:T(8,128)(2,1)} %bitcast.11, bf16[16,64,128]{2,1,0:T(8,128)(2,1)} %bitcast.12, bf16[64,192]{1,0:T(8,128)(2,1)} %bitcast.14, ...), custom_call_target="tpu_custom_call" | custom-call | tf_op jit(solution)/shard_map/pallas_call | solution.py:695
  47.2 0.7 %copy.11 = bf16[128,640]{1,0:T(8,128)(2,1)} copy(bf16[128,640]{1,0:T(8,128)(2,1)S(1)} %shard_map.91) | data formatting | bytes 327680

commit v5 on v4

--- a/solution.py
+++ b/solution.py
@@ -147,9 +147,9 @@
     span = 2 * TILE
     half = n // 2
     chips = n // 2
-    staged = len(late) == 2
+    staged = len(late) > 0
     ready = early.shape[0]
-    batch = ready // 6
+    starts = [ready, ready + 4, ready + 6]
     side = me // half
     outer = (me < half - 2) | (me >= half + 2)
 
@@ -283,7 +283,8 @@
         if not staged:
             target = early.at[step * cap + slot]
         elif late_one:
-            target = late[slot // 2].at[lax.rem(step, 2) * 2 + slot % 2]
+            odd = lax.rem(step, 2)
+            target = late[0].at[odd * 2 + slot] if slot < 2 else late[slot - 1].at[odd]
         else:
             place = jnp.where(step < half, step, half + lax.rem(step, 2))
             target = early.at[place * cap + slot]
@@ -425,17 +426,20 @@
     def rank(step, carry):
         owner = flip(me, step, n)
         if not staged:
-            order_smem[0, owner] = step * cap
-            order_smem[1, owner] = 0
+            for line, value in enumerate([step * cap, step * cap, 1]):
+                order_smem[line, owner] = value
         else:
-            inner = (owner >= half - 2) & (owner < half + 2)
-            last = (step >= half) & inner
-            place = jnp.where(step < half, step, half + lax.rem(step, 2))
-            order_smem[0, owner] = jnp.where(last, ready + lax.rem(step, 2) * 2, place * cap)
-            order_smem[1, owner] = jnp.where(last, batch - 2, 0)
+            central = (owner >= half - 2) & (owner < half + 2)
+            last = (step >= half) & central
+            odd = lax.rem(step, 2)
+            place = jnp.where(step < half, step, half + odd) * cap
+            order_smem[0, owner] = jnp.where(last, ready + odd * 2, place)
+            order_smem[1, owner] = jnp.where(last, ready + odd, place)
+            order_smem[2, owner] = jnp.where(last, 2, 1)
         return carry
 
     lax.fori_loop(0, n, rank, 0)
+    newest = (context - TILE * n + me * TILE) // (blocks * BLK)
     entries = [own_smem[0, 0, entry] for entry in range(SEL)]
     owners = [entry // blocks for entry in entries]
     marks = []
@@ -443,8 +447,12 @@
         slot = jnp.int32(0)
         for other in range(entry):
             slot = slot + (owners[other] == owners[entry]).astype(jnp.int32)
-        place = order_smem[0, owners[entry]] + slot
-        place = place + jnp.where(slot >= 2, order_smem[1, owners[entry]], 0)
+        place = jnp.where(
+            slot < 2,
+            order_smem[0, owners[entry]] + slot,
+            order_smem[1, owners[entry]] + slot * order_smem[2, owners[entry]],
+        )
+        place = jnp.where(owners[entry] == newest, place, place + n * cap)
         marks.append(place * MARK + entries[entry])
     for low, high in exchanges(SEL):
         marks[low], marks[high] = (
@@ -452,7 +460,7 @@
             jnp.maximum(marks[low], marks[high]),
         )
     for entry in range(SEL):
-        order_smem[2, entry] = marks[entry]
+        order_smem[3, entry] = marks[entry]
     mine = picks(lambda entry: own_smem[0, 0, entry], me, blocks, cap)
     for slot in range(cap):
         early[slot] = packed[jnp.maximum(mine[slot] - me * blocks, 0)]
@@ -472,7 +480,22 @@
         keys_wide[place * BLK : (place + 1) * BLK] = keys
         return values
 
-    def attend(count, bounds, stride, top_ref, sum_ref, out, first):
+    def gate_row(index, kind):
+        first_head = kind * heads + index * (span // TILE)
+        return jnp.concatenate(
+            [gates[first_head + other : first_head + other + 1] for other in range(span // TILE)],
+            axis=1,
+        )
+
+    def close(index, picked, total):
+        here = slice(index * span, (index + 1) * span)
+        mixed = coarse_out[:, here] + picked * (gate_row(index, 1) / total)
+        mixed = mixed.astype(jnp.bfloat16)
+        for other in range(span // TILE):
+            start = index * span + other * TILE
+            attended[:, start : start + TILE] = mixed[:, other * TILE : (other + 1) * TILE].T
+
+    def attend(count, bounds, stride, top_ref, sum_ref, out, first, closing=False):
         lag = row * stride - query
         total = heads * TILE // span
 
@@ -484,13 +507,14 @@
 
         def soft(index, scores):
             here = slice(index * span, (index + 1) * span)
-            scores = jnp.concatenate(
-                [
-                    jnp.where(lag <= bounds[block], scores[block * BLK : (block + 1) * BLK], -jnp.inf)
-                    for block in range(count)
-                ],
-                axis=0,
-            )
+            if bounds is not None:
+                scores = jnp.concatenate(
+                    [
+                        jnp.where(lag <= bounds[block], scores[block * BLK : (block + 1) * BLK], -jnp.inf)
+                        for block in range(count)
+                    ],
+                    axis=0,
+                )
             top = jnp.max(scores, axis=0, keepdims=True)
             if first:
                 new = jnp.maximum(top, NEGATIVE)
@@ -499,7 +523,8 @@
                 old = top_ref[:, here]
                 new = jnp.maximum(old, top)
                 factor = jnp.exp2((old - new) * scale)
-            top_ref[:, here] = new
+            if not closing:
+                top_ref[:, here] = new
             return jnp.exp2((scores - new) * scale).astype(jnp.bfloat16), factor
 
         def value(index, exponents, factor):
@@ -510,6 +535,12 @@
             if first:
                 out[:, here] = added[:128]
                 sum_ref[:, here] = added[128:129]
+            elif closing:
+                close(
+                    index,
+                    out[:, here] * factor + added[:128],
+                    sum_ref[:, here] * factor + added[128:129],
+                )
             else:
                 out[:, here] = out[:, here] * factor + added[:128]
                 sum_ref[:, here] = sum_ref[:, here] * factor + added[128:129]
@@ -523,20 +554,26 @@
     values_wide[128:, :] = jnp.ones_like(values_wide[128:, :])
 
     def gather(mark, turn):
-        place = mark // MARK
+        place = lax.rem(mark // MARK, n * cap)
         block = early[jnp.minimum(place, ready - 1)]
         for index in range(turn):
-            start = ready + index * batch
-            other = late[index][jnp.clip(place - start, 0, batch - 1)]
-            block = jnp.where(place >= start, other, block)
+            other = late[index]
+            start = starts[index]
+            block = jnp.where(
+                place >= start, other[jnp.clip(place - start, 0, other.shape[0] - 1)], block
+            )
         return block
 
-    def attend_picked(turn, start):
-        marks = [order_smem[2, start + index] for index in range(PART)]
+    def attend_picked(turn, start, count, closing=False):
+        marks = [order_smem[3, start + index] for index in range(count)]
         values = [fill(index, gather(mark, turn)) for index, mark in enumerate(marks)]
-        values_wide[:128, : PART * BLK] = jnp.concatenate(values, axis=0).T
-        bounds = [first_pos - lax.rem(mark, MARK) * BLK for mark in marks]
-        attend(PART, bounds, 1, picked_top, picked_sum, picked_out, start == 0)
+        values_wide[:128, : count * BLK] = jnp.concatenate(values, axis=0).T
+        bounds = None
+        if start == 0:
+            bounds = [first_pos - lax.rem(mark, MARK) * BLK for mark in marks]
+        attend(
+            count, bounds, 1, picked_top, picked_sum, picked_out, start == 0, closing
+        )
 
     loads[5].wait()
     loads[6].wait()
@@ -573,6 +610,10 @@
 
         lax.fori_loop(1, n // pieces, coarse_more, 0)
 
+    for index in range(heads * TILE // span):
+        here = slice(index * span, (index + 1) * span)
+        coarse_out[:, here] = coarse_out[:, here] * (gate_row(index, 0) / coarse_sum[:, here])
+
     def wait_slots(start, stop, slots, late_one, base=None):
         def wait_one(index, carry):
             step = index if base is None else flip(me, base + index, n)
@@ -585,22 +626,18 @@
     if not staged:
         wait_slots(1, n, range(cap), False)
         for start in range(0, SEL, PART):
-            attend_picked(0, start)
+            attend_picked(0, start, PART, start + PART == SEL)
     else:
         wait_slots(1, half, range(cap), False)
         wait_slots(0, 2, range(cap), False, (n - 2) * (1 - side))
         for start in range(0, SEL // 2, PART):
-            attend_picked(0, start)
-        for turn in range(2):
-            wait_slots(0, 2, range(turn * 2, turn * 2 + 2), True, half - 2 * side)
-            attend_picked(turn + 1, SEL // 2 + turn * PART)
-
-    for head in range(heads):
-        here = slice(head * 128, (head + 1) * 128)
-        of_coarse = gates[head : head + 1] / coarse_sum[:, here]
-        of_picked = gates[heads + head : heads + head + 1] / picked_sum[:, here]
-        mixed = coarse_out[:, here] * of_coarse + picked_out[:, here] * of_picked
-        attended[:, here] = mixed.T.astype(jnp.bfloat16)
+            attend_picked(0, start, PART)
+        start = SEL // 2
+        for turn, slots in enumerate([range(2), range(2, 3), range(3, 4)]):
+            wait_slots(0, 2, slots, True, half - 2 * side)
+            count = 2 * len(slots)
+            attend_picked(turn + 1, start, count, turn == 2)
+            start += count
 
     def part_copy(step):
         return pltpu.make_async_remote_copy(
@@ -677,7 +714,7 @@
     columns = out_weight.shape[1] // groups
     pieces = min(n, 8)
     wide = max(pieces, PART) * BLK
-    staged = n == 8 and cap == 4
+    staged = n == 8 and cap == 4 and n * TILE <= ctx_dev
 
     vmem = pl.BlockSpec(memory_space=pltpu.VMEM)
     hbm = pl.BlockSpec(memory_space=pl.ANY)
@@ -702,10 +739,10 @@
             pltpu.VMEM((blocks, UNIT, 128), bf16),
             pltpu.VMEM((256, rows), bf16),
             pltpu.SMEM((n, 1, 1, SEL), jnp.int32),
-            pltpu.SMEM((3, max(n, SEL)), jnp.int32),
+            pltpu.SMEM((4, max(n, SEL)), jnp.int32),
             pltpu.VMEM((n, cap, UNIT, 128), bf16),
             pltpu.VMEM(((n - 2 * staged) * cap, UNIT, 128), bf16),
-            [pltpu.VMEM((cap, UNIT, 128), bf16) for _ in range(2 * staged)],
+            [pltpu.VMEM((size, UNIT, 128), bf16) for size in ([4, 2, 2] if staged else [])],
             pltpu.VMEM((n, UNIT, 128), bf16),
             pltpu.VMEM((wide, 256), bf16),
             pltpu.VMEM((144, wide), bf16),

time: 48 us -> 47.5 us (0.990)
  Pallas kernels: 47.2 us -> 46.7 us
    pallas_call x1, Pallas kernels: 47.2 us -> 46.7 us  [shards(): pl.pallas_call(functools.partial(kernel, n, groups, cap, width ** (-0.5)...]
where the time goes in v5:
time: 47.5 us; the launch traced here: 47.3 us
  Pallas kernels  46.7 us (98%)
  local copies, waits for them, and re-layouts  0.67 us (1%)
    pallas_call x1, Pallas kernels, shards(): pl.pallas_call(functools.partial(kernel, n, groups, cap, width ** (-0.5)...  46.7 us

profile of v5, /device:TPU:0, one launch (start us, length us, event | category | flops | bytes accessed | tf_op | source)
XLA Modules:
  0.0 47.3 jit_solution(8941776769187778679)
XLA Ops:
  0.0 46.7 %shard_map.91 = bf16[128,640]{1,0:T(8,128)(2,1)S(1)} custom-call(s32[1,1,16]{2,1,0:T(1,128)} %own_table.1, s32[1,1,16]{2,1,0:T(1,128)} %own_table.1, bf16[16,192,128]{2,1,0:T(8,128)(2,1)} %bitcast.10, bf16[192,1024]{1,0:T(8,128)(2,1)} %bitcast.11, bf16[16,64,128]{2,1,0:T(8,128)(2,1)} %bitcast.12, bf16[64,192]{1,0:T(8,128)(2,1)} %bitcast.14, ...), custom_call_target="tpu_custom_call" | custom-call | tf_op jit(solution)/shard_map/pallas_call | solution.py:732
  46.7 0.7 %copy.11 = bf16[128,640]{1,0:T(8,128)(2,1)} copy(bf16[128,640]{1,0:T(8,128)(2,1)S(1)} %shard_map.91) | data formatting | bytes 327680

commit v6 on v5

--- a/solution.py
+++ b/solution.py
@@ -333,6 +333,9 @@
     def far_step(phase, chip):
         return flip(me, half - side + (1 - 2 * side) * (2 * chip + phase), n)
 
+    def useful(owner, tile, slot):
+        return (owner * blocks + slot) * BLK < context - TILE * n + (tile + 1) * TILE
+
     def send_far(phase, first, last):
         def fill_far(chip, carry):
             fill_slots(far_step(phase, chip))
@@ -349,22 +352,31 @@
 
             lax.fori_loop(0, half // 2, send_single, 0)
             return
-        lag = 1.5 if phase else -0.1
-        order = [
-            (slot + lag * (half // 2 - 1 - chip), chip, slot)
-            for chip in range(first, last)
-            for slot in range(cap)
-        ]
-        for _, chip, slot in sorted(order):
-            step = far_step(phase, chip)
-
-            @pl.when(outer)
-            def _():
-                slot_copy(step, slot, False).start()
-
-            @pl.when(inner)
-            def _():
-                slot_copy(step, slot, True).start()
+        def send_order(lag, late_one):
+            order = [
+                (slot + lag * (half // 2 - 1 - chip), chip, slot)
+                for chip in range(first, last)
+                for slot in range(cap)
+            ]
+            for _, chip, slot in sorted(order):
+                step = far_step(phase, chip)
+                copy = slot_copy(step, slot, late_one)
+                if slot < 2 or late_one:
+                    copy.start()
+                else:
+                    pl.when(useful(me, flip(me, step, n), slot))(copy.start)
+
+        @pl.when(outer)
+        def _():
+            send_order(1.5 if phase else -0.1, False)
+
+        @pl.when(inner & (side == 0))
+        def _():
+            send_order(0.7 if phase else -0.1, True)
+
+        @pl.when(inner & (side == 1))
+        def _():
+            send_order(1.5 if phase else -0.1, True)
 
     def send_chip(start, stop):
         lax.fori_loop(start, stop, send_near, 0)
@@ -555,7 +567,7 @@
 
     def gather(mark, turn):
         place = lax.rem(mark // MARK, n * cap)
-        block = early[jnp.minimum(place, ready - 1)]
+        block = early[jnp.where(place < ready, place, 0)]
         for index in range(turn):
             other = late[index]
             start = starts[index]
@@ -618,7 +630,11 @@
         def wait_one(index, carry):
             step = index if base is None else flip(me, base + index, n)
             for slot in slots:
-                slot_copy(step, slot, late_one).wait_recv()
+                copy = slot_copy(step, slot, late_one)
+                if base is None or slot < 2 or late_one:
+                    copy.wait_recv()
+                else:
+                    pl.when(useful(flip(me, step, n), me, slot))(copy.wait_recv)
             return carry
 
         lax.fori_loop(start, stop, wait_one, 0)
@@ -639,22 +655,27 @@
             attend_picked(turn + 1, start, count, turn == 2)
             start += count
 
-    def part_copy(step):
+    halves = [(0, columns // 256 * 128), (columns // 256 * 128, columns)]
+
+    def part_copy(step, half_of):
+        here = slice(*halves[half_of])
         return pltpu.make_async_remote_copy(
-            src_ref=partial.at[step],
-            dst_ref=arrived.at[step],
-            send_sem=part_send.at[step],
-            recv_sem=part_recv.at[step],
+            src_ref=partial.at[step, :, here],
+            dst_ref=arrived.at[step, :, here],
+            send_sem=part_send.at[step, half_of],
+            recv_sem=part_recv.at[step, half_of],
             device_id={"grp": flip(group, step, groups)},
             device_id_type=MESH,
         )
 
     for step in reversed(range(1, groups)):
         weight_copy(step).wait()
-        partial[step] = jnp.dot(
-            attended[...], weights[step], preferred_element_type=jnp.float32
-        ).astype(jnp.bfloat16)
-        part_copy(step).start()
+        for half_of in range(2):
+            here = slice(*halves[half_of])
+            partial[step, :, here] = jnp.dot(
+                attended[...], weights[step, :, here], preferred_element_type=jnp.float32
+            ).astype(jnp.bfloat16)
+            part_copy(step, half_of).start()
     weight_copy(0).wait()
     own_part[...] = jnp.dot(attended[...], weights[0], preferred_element_type=jnp.float32)
 
@@ -666,7 +687,11 @@
 
     def sent_slots(step, carry):
         for slot in range(cap):
-            slot_copy(step, slot, False).wait_send()
+            copy = slot_copy(step, slot, False)
+            if slot < 2 or not staged:
+                copy.wait_send()
+            else:
+                pl.when(useful(me, flip(me, step, n), slot))(copy.wait_send)
         return carry
 
     lax.fori_loop(1, n, sent_slots, 0)
@@ -684,11 +709,13 @@
 
     total = own_part[...]
     for step in range(1, groups):
-        part_copy(step).wait_recv()
+        for half_of in range(2):
+            part_copy(step, half_of).wait_recv()
         total = total + arrived[step].astype(jnp.float32)
     out_ref[...] = total.astype(out_ref.dtype)
     for step in range(1, groups):
-        part_copy(step).wait_send()
+        for half_of in range(2):
+            part_copy(step, half_of).wait_send()
 
 
 def shards(
@@ -767,8 +794,8 @@
             dma((n // 2,)),
             dma((n // 2,)),
             dma((n // 2,)),
-            dma((groups,)),
-            dma((groups,)),
+            dma((groups, 2)),
+            dma((groups, 2)),
             pltpu.SemaphoreType.REGULAR((2,)),
         ],
         compiler_params=pltpu.CompilerParams(

time: 47.5 us -> 46.9 us (0.987)
  Pallas kernels: 46.7 us -> 46.1 us
    pallas_call x1, Pallas kernels: 46.7 us -> 46.1 us  [shards(): pl.pallas_call(functools.partial(kernel, n, groups, cap, width ** (-0.5)...]
where the time goes in v6:
time: 46.9 us; the launch traced here: 46.8 us
  Pallas kernels  46.1 us (98%)
  local copies, waits for them, and re-layouts  0.67 us (1%)
    pallas_call x1, Pallas kernels, shards(): pl.pallas_call(functools.partial(kernel, n, groups, cap, width ** (-0.5)...  46.1 us

profile of v6, /device:TPU:0, one launch (start us, length us, event | category | flops | bytes accessed | tf_op | source)
XLA Modules:
  0.0 46.8 jit_solution(3424984970938276538)
XLA Ops:
  0.0 46.1 %shard_map.91 = bf16[128,640]{1,0:T(8,128)(2,1)S(1)} custom-call(s32[1,1,16]{2,1,0:T(1,128)} %own_table.1, s32[1,1,16]{2,1,0:T(1,128)} %own_table.1, bf16[16,192,128]{2,1,0:T(8,128)(2,1)} %bitcast.10, bf16[192,1024]{1,0:T(8,128)(2,1)} %bitcast.11, bf16[16,64,128]{2,1,0:T(8,128)(2,1)} %bitcast.12, bf16[64,192]{1,0:T(8,128)(2,1)} %bitcast.14, ...), custom_call_target="tpu_custom_call" | custom-call | tf_op jit(solution)/shard_map/pallas_call | solution.py:759
  46.1 0.7 %copy.11 = bf16[128,640]{1,0:T(8,128)(2,1)} copy(bf16[128,640]{1,0:T(8,128)(2,1)S(1)} %shard_map.91) | data formatting | bytes 327680

commit v7 on v6

--- a/solution.py
+++ b/solution.py
@@ -376,7 +376,7 @@
 
         @pl.when(inner & (side == 1))
         def _():
-            send_order(1.5 if phase else -0.1, True)
+            send_order(2.5 if phase else -0.1, True)
 
     def send_chip(start, stop):
         lax.fori_loop(start, stop, send_near, 0)
@@ -668,14 +668,18 @@
             device_id_type=MESH,
         )
 
-    for step in reversed(range(1, groups)):
+    for step in range(1, groups):
         weight_copy(step).wait()
-        for half_of in range(2):
-            here = slice(*halves[half_of])
-            partial[step, :, here] = jnp.dot(
-                attended[...], weights[step, :, here], preferred_element_type=jnp.float32
-            ).astype(jnp.bfloat16)
-            part_copy(step, half_of).start()
+    last = groups - 1
+    turns = [(last, 0), (last - 1, 0), (last, 1)]
+    turns += [(step, half_of) for step in range(1, last - 1) for half_of in range(2)]
+    turns += [(last - 1, 1)]
+    for step, half_of in turns:
+        here = slice(*halves[half_of])
+        partial[step, :, here] = jnp.dot(
+            attended[...], weights[step, :, here], preferred_element_type=jnp.float32
+        ).astype(jnp.bfloat16)
+        part_copy(step, half_of).start()
     weight_copy(0).wait()
     own_part[...] = jnp.dot(attended[...], weights[0], preferred_element_type=jnp.float32)
 

time: 46.9 us -> 46.2 us (0.985)
  Pallas kernels: 46.1 us -> 45.4 us
    pallas_call x1, Pallas kernels: 46.1 us -> 45.4 us  [shards(): pl.pallas_call(functools.partial(kernel, n, groups, cap, width ** (-0.5)...]
where the time goes in v7:
time: 46.2 us; the launch traced here: 46 us
  Pallas kernels  45.4 us (98%)
  local copies, waits for them, and re-layouts  0.67 us (1%)
    pallas_call x1, Pallas kernels, shards(): pl.pallas_call(functools.partial(kernel, n, groups, cap, width ** (-0.5)...  45.4 us

profile of v7, /device:TPU:0, one launch (start us, length us, event | category | flops | bytes accessed | tf_op | source)
XLA Modules:
  0.0 46.0 jit_solution(9984732765430702084)
XLA Ops:
  0.0 45.4 %shard_map.91 = bf16[128,640]{1,0:T(8,128)(2,1)S(1)} custom-call(s32[1,1,16]{2,1,0:T(1,128)} %own_table.1, s32[1,1,16]{2,1,0:T(1,128)} %own_table.1, bf16[16,192,128]{2,1,0:T(8,128)(2,1)} %bitcast.10, bf16[192,1024]{1,0:T(8,128)(2,1)} %bitcast.11, bf16[16,64,128]{2,1,0:T(8,128)(2,1)} %bitcast.12, bf16[64,192]{1,0:T(8,128)(2,1)} %bitcast.14, ...), custom_call_target="tpu_custom_call" | custom-call | tf_op jit(solution)/shard_map/pallas_call | solution.py:763
  45.4 0.7 %copy.11 = bf16[128,640]{1,0:T(8,128)(2,1)} copy(bf16[128,640]{1,0:T(8,128)(2,1)S(1)} %shard_map.91) | data formatting | bytes 327680

commit v8 on v7

--- a/solution.py
+++ b/solution.py
@@ -400,9 +400,9 @@
 
             coarse_pass(3)
             hop(3).start()
+            send_far(0, 1, 2)
             coarse_pass(1)
             hop(2).start()
-            send_far(0, 1, 2)
             coarse_pass(2)
             hop(4).start()
 

time: 46.2 us -> 45.9 us (level); the launches traced: 46 us -> 45 us
  Pallas kernels: 45.4 us -> 44.4 us
    pallas_call x1, Pallas kernels: 45.4 us -> 44.4 us  [shards(): pl.pallas_call(functools.partial(kernel, n, groups, cap, width ** (-0.5)...]
where the time goes in v8:
time: 45.9 us; the launch traced here: 45 us
  Pallas kernels  44.4 us (97%)
  local copies, waits for them, and re-layouts  0.67 us (1%)
    pallas_call x1, Pallas kernels, shards(): pl.pallas_call(functools.partial(kernel, n, groups, cap, width ** (-0.5)...  44.4 us

profile of v8, /device:TPU:0, one launch (start us, length us, event | category | flops | bytes accessed | tf_op | source)
XLA Modules:
  0.0 45.0 jit_solution(1072444256695551279)
XLA Ops:
  0.0 44.4 %shard_map.91 = bf16[128,640]{1,0:T(8,128)(2,1)S(1)} custom-call(s32[1,1,16]{2,1,0:T(1,128)} %own_table.1, s32[1,1,16]{2,1,0:T(1,128)} %own_table.1, bf16[16,192,128]{2,1,0:T(8,128)(2,1)} %bitcast.10, bf16[192,1024]{1,0:T(8,128)(2,1)} %bitcast.11, bf16[16,64,128]{2,1,0:T(8,128)(2,1)} %bitcast.12, bf16[64,192]{1,0:T(8,128)(2,1)} %bitcast.14, ...), custom_call_target="tpu_custom_call" | custom-call | tf_op jit(solution)/shard_map/pallas_call | solution.py:763
  44.4 0.7 %copy.11 = bf16[128,640]{1,0:T(8,128)(2,1)} copy(bf16[128,640]{1,0:T(8,128)(2,1)S(1)} %shard_map.91) | data formatting | bytes 327680

commit v9 on v8

--- a/solution.py
+++ b/solution.py
@@ -398,9 +398,9 @@
             def _():
                 send_chip(2, half)
 
+            send_far(0, 1, 2)
             coarse_pass(3)
             hop(3).start()
-            send_far(0, 1, 2)
             coarse_pass(1)
             hop(2).start()
             coarse_pass(2)

time: 45.9 us -> 45.9 us (level)
  no operation moved by 1% of the time
where the time goes in v9:
time: 45.9 us; the launch traced here: 45 us
  Pallas kernels  44.4 us (97%)
  local copies, waits for them, and re-layouts  0.67 us (1%)
    pallas_call x1, Pallas kernels, shards(): pl.pallas_call(functools.partial(kernel, n, groups, cap, width ** (-0.5)...  44.4 us

profile of v9, /device:TPU:0, one launch (start us, length us, event | category | flops | bytes accessed | tf_op | source)
XLA Modules:
  0.0 45.0 jit_solution(17088425983998938955)
XLA Ops:
  0.0 44.4 %shard_map.91 = bf16[128,640]{1,0:T(8,128)(2,1)S(1)} custom-call(s32[1,1,16]{2,1,0:T(1,128)} %own_table.1, s32[1,1,16]{2,1,0:T(1,128)} %own_table.1, bf16[16,192,128]{2,1,0:T(8,128)(2,1)} %bitcast.10, bf16[192,1024]{1,0:T(8,128)(2,1)} %bitcast.11, bf16[16,64,128]{2,1,0:T(8,128)(2,1)} %bitcast.12, bf16[64,192]{1,0:T(8,128)(2,1)} %bitcast.14, ...), custom_call_target="tpu_custom_call" | custom-call | tf_op jit(solution)/shard_map/pallas_call | solution.py:763
  44.4 0.7 %copy.11 = bf16[128,640]{1,0:T(8,128)(2,1)} copy(bf16[128,640]{1,0:T(8,128)(2,1)S(1)} %shard_map.91) | data formatting | bytes 327680
